TPU v7x, 32 devices: a whole 2x2x4 slice. The times are simulated.
32 devices in a mesh: row: 8 (over y, x, core), col: 4 (over z).
Axes of the slice: x: 2, y: 2, z: 4, core: 2. Of those that a mesh axis runs over, the one named last changes fastest.
Arguments:
- alpha_prev: float32 [48, 4096], P(None, 'row'), may hold values from 0.1 to 10
- tokens: int32 [48], replicated, may hold values from 0 to 16639
- src_emb: bfloat16 [4096, 256], P('row'), may hold values from -10 to 10
- dst_emb: bfloat16 [256, 4096], P(None, ('row', 'col')), may hold values from -7 to 7
- emission: bfloat16 [16640, 4096], P(None, ('row', 'col')), may hold values from 0.02 to 8, as said below
Outputs:
- next_alpha: float32 [48, 4096], P(None, 'row')
- log_total: float32 [48], replicated
Inputs may be any that keep to these rules, and one draw needn't show every extreme that they name: `emission`: every weight is positive.
All inputs are finite; a program needn't handle non-finite values.
Results may differ from a plain program's by a relative error of at most 0.0014.
Values may be sent and summed in bfloat16 or wider, within the bound.
No kernel may reach another device: no remote copies, remote signals or barrier semaphores. Data moves between devices by JAX's collectives and lax.ppermute only.
A program may use at most 128 MiB of HBM per device.

v0:
```python
import math
import jax
import jax.numpy as jnp
from jax import lax
from jax.sharding import PartitionSpec as P


def absorb(folded, sources, shard_piece, group_cols):
    src_rows = sources.shape[0]
    piece_groups = shard_piece.shape[1] // group_cols
    per_turn = math.gcd(piece_groups, max(1, (1 << 20) // (src_rows * group_cols)))

    def absorb_block(turn_index, tile_state):
        expo_tile, part_peak, part_total = tile_state
        offset = turn_index * (per_turn * group_cols)
        columns = lax.dynamic_slice_in_dim(shard_piece, offset, per_turn * group_cols, 1)
        logits = jnp.dot(sources, columns, preferred_element_type=jnp.float32).reshape(
            src_rows, per_turn, group_cols
        )
        block_peak = jnp.max(logits, axis=2)
        shifted = jnp.exp(logits - block_peak[:, :, None])
        block_total = jnp.sum(shifted, axis=2)
        expo_block = shifted.reshape(src_rows, per_turn * group_cols).astype(jnp.bfloat16)
        expo_tile = lax.dynamic_update_slice_in_dim(expo_tile, expo_block, offset, 1)
        group_slot = turn_index * per_turn
        part_peak = lax.dynamic_update_slice_in_dim(part_peak, block_peak, group_slot, 1)
        part_total = lax.dynamic_update_slice_in_dim(part_total, block_total, group_slot, 1)
        return (expo_tile, part_peak, part_total)

    return lax.fori_loop(0, piece_groups // per_turn, absorb_block, folded)


def start_state(src_rows, tile_cols, group_cols):
    groups = tile_cols // group_cols
    return (
        jnp.zeros((src_rows, tile_cols), jnp.bfloat16),
        jnp.zeros((src_rows, groups), jnp.float32),
        jnp.zeros((src_rows, groups), jnp.float32),
    )


def on_device(alpha_prev, tokens, src_emb, dst_emb, emission):
    group_cols = dst_emb.shape[1]
    row_count = lax.axis_size("row")
    col_count = lax.axis_size("col")
    seq_count = alpha_prev.shape[0]
    row_index = lax.axis_index("row")
    tile_cols = group_cols * row_count
    folded = absorb(
        start_state(src_emb.shape[0], tile_cols, group_cols),
        src_emb,
        lax.all_gather(dst_emb, "row", axis=1, tiled=True),
        group_cols,
    )
    expo_tile, part_peak, part_total = folded
    src_rows = src_emb.shape[0]
    local_peak = jnp.max(part_peak, axis=1)
    local_total = jnp.sum(part_total * jnp.exp(part_peak - local_peak[:, None]), axis=1)
    row_peak = lax.pmax(local_peak, "col")
    row_total = lax.psum(local_total * jnp.exp(local_peak - row_peak), "col")
    row_scale = jnp.exp(part_peak - row_peak[:, None]) / row_total[:, None]
    local_groups = tile_cols // group_cols
    per_block = math.gcd(local_groups, 16)

    def multiply(block_index, partial_value):
        group_start = block_index * per_block
        scale_cols = lax.dynamic_slice_in_dim(row_scale, group_start, per_block, 1)
        weights = (scale_cols.T[:, None, :] * alpha_prev[None, :, :]).astype(jnp.bfloat16)
        expo_cols = lax.dynamic_slice_in_dim(
            expo_tile, group_start * group_cols, per_block * group_cols, 1
        ).reshape(src_rows, per_block, group_cols)
        product = jnp.einsum("gbi,igk->bgk", weights, expo_cols, preferred_element_type=jnp.float32)
        return lax.dynamic_update_slice_in_dim(
            partial_value,
            product.reshape(seq_count, per_block * group_cols),
            group_start * group_cols,
            1,
        )

    partial_value = lax.fori_loop(
        0, local_groups // per_block, multiply, jnp.zeros((seq_count, tile_cols), jnp.float32)
    )
    summed = lax.psum(partial_value, "row")
    own_sums = lax.dynamic_slice_in_dim(summed, row_index * group_cols, group_cols, 1)
    emit_rows = jnp.take(emission, tokens, axis=0).astype(jnp.float32)
    emitted = own_sums * emit_rows
    state_count = float(group_cols * row_count * col_count)
    total = lax.psum(jnp.sum(emitted, axis=1), ("row", "col"))
    scaled = emitted * (state_count / total)[:, None]
    next_alpha = lax.all_gather(scaled, "col", axis=1, tiled=True)
    log_total = jnp.log(total)
    return (next_alpha, log_total)


def solution(mesh):
    placed = (P(None, "row"), P(), P("row", None), P(None, ("row", "col")), P(None, ("row", "col")))
    return jax.shard_map(
        on_device, mesh=mesh, in_specs=placed, out_specs=(P(None, "row"), P()), check_vma=False
    )
```

profile of v0, /device:TPU:0, one launch (start us, length us, event | category | flops | bytes accessed | tf_op | source)
XLA Modules:
  0.0 166.4 jit_solution(14309806764282524219)
XLA Ops:
  7.2 0.0 copy-start
  7.2 0.0 all-reduce.2.cloned.1.call-start
  7.2 11.9 %all_gather.6 = bf16[256,1024]{1,0:T(8,128)(2,1)S(1)} all-gather(bf16[256,128]{1,0:T(8,128)(2,1)} %param.8), channel_id=1, replica_groups=mesh['row'=8,'col'=4] {'row'}, dimensions={1}, use_global_device_ids=true | all-gather | bytes 589824 | tf_op jit(solution)/shard_map/all_gather | solution.py:52
  19.1 0.0 copy-done
  19.1 0.4 fusion.11
  19.5 1.8 %copy.20 = f32[64,8,8,128]{3,2,1,0:T(8,128)} copy(f32[64,8,8,128]{3,1,2,0:T(8,128)S(1)} %bitcast.26) | data formatting | bytes 4194304
  21.3 2.2 %reduce_max.19 = f32[512,8]{1,0:T(8,128)S(1)} reduce(f32[512,8,128]{2,1,0:T(8,128)} %bitcast.27, f32[]{:T(128)} %constant.29.clone.1), dimensions={2}, to_apply=%region_0.1 | reduce | flops 520192 | bytes 2113540 | tf_op jit(solution)/shard_map/while/body/eval_jaxpr/reduce_max | solution.py:20
  23.6 2.8 %exponential_reduce_fusion = f32[512,8]{1,0:T(8,128)S(1)} fusion(f32[512,8,128]{2,1,0:T(8,128)} %bitcast.28, f32[512,8]{1,0:T(8,128)S(1)} %reduce_max.19), kind=kLoop, calls=%fused_computation.4 | loop fusion | flops 1044480 | bytes 2129920 | tf_op jit(solution)/shard_map/while/body/eval_jaxpr/reduce_sum | solution.py:22
  26.4 0.1 copy.15
  26.5 0.6 sub.38
  27.1 0.0 copy-start.1
  27.1 1.5 fusion.9
  28.6 0.0 copy-start.2
  28.6 12.1 %pmax.7 = f32[512]{0:T(512)S(1)} all-reduce(f32[512]{0:T(512)S(1)} %get-tuple-element.29), channel_id=1, replica_groups=mesh['row'=8,'col'=4] {'col'}, use_global_device_ids=true, to_apply=%region_2.3 | all-reduce | flops 512 | bytes 4096 | tf_op jit(solution)/shard_map/pmax | solution.py:59
  40.7 0.2 multiply_reduce_fusion
  41.0 8.4 %psum.21 = f32[512]{0:T(512)S(1)} all-reduce(f32[512]{0:T(512)S(1)} %exponential_multiply_fusion), channel_id=1, replica_groups=mesh['row'=8,'col'=4] {'col'}, use_global_device_ids=true, to_apply=%region_5.0 | all-reduce | flops 512 | bytes 4096 | tf_op jit(solution)/shard_map/psum | solution.py:60
  49.4 0.0 copy-done.1
  49.4 1.6 convolution_bitcast_fusion
  51.0 0.7 copy.30
  51.7 0.0 all-reduce.2.cloned.1.call-update
  51.7 0.0 copy-done.2
  51.8 3.3 %gather_fusion = bf16[48,128]{1,0:T(8,128)(2,1)S(1)} fusion(bf16[16640,128]{1,0:T(8,128)(2,1)} %param.9, s32[1024]{0:T(1024)S(1)} %pad_clamp_fusion), kind=kCustom, calls=%fused_computation | custom fusion | bytes 24768 | tf_op jit(solution)/shard_map/jit(_take)/gather | solution.py:85
  55.1 48.8 %all-reduce.2.cloned.1.call-done = f32[48,1024]{1,0:T(8,128)} async-done(((f32[48,1024]{1,0:T(8,128)}), f32[48,1024]{1,0:T(8,128)}) %all-reduce.2.cloned.1.call-update) | async-done | bytes 196624 | tf_op jit(solution)/shard_map/psum | solution.py:83
  103.9 0.9 fusion.8
  104.8 39.3 %psum.23 = f32[48]{0:T(128)S(1)} all-reduce(f32[48]{0:T(128)S(1)} %fusion.8), channel_id=1, replica_groups=mesh['row'=8,'col'=4] {'row','col'}, use_global_device_ids=true, to_apply=%region_8.0 | all-reduce | flops 48 | bytes 384 | tf_op jit(solution)/shard_map/psum | solution.py:88
  144.2 0.5 fusion.10
  144.7 0.8 fusion.7
  145.5 13.3 %all_gather.7 = f32[48,512]{1,0:T(8,128)S(1)} all-gather(f32[48,128]{1,0:T(8,128)S(1)} %fusion.7), channel_id=1, replica_groups=mesh['row'=8,'col'=4] {'col'}, dimensions={1}, use_global_device_ids=true | all-gather | bytes 122880 | tf_op jit(solution)/shard_map/all_gather | solution.py:90
  158.9 0.6 copy.33
  (5 shorter events, 0.0 us)
Async XLA Ops:
  7.2 11.9 %copy-start = (bf16[512,256]{1,0:T(8,128)(2,1)S(1)}, bf16[512,256]{1,0:T(8,128)(2,1)}, u32[]{:S(2)}) copy-start(bf16[512,256]{1,0:T(8,128)(2,1)} %param.7) | copy-start | bytes 786436
  7.2 96.7 %all-reduce.2.cloned.1.call-start = ((), (), s32[]{:S(2)}) async-start(), calls=%async_computation | async-start | bytes 393216 | tf_op jit(solution)/shard_map/psum | solution.py:83
  27.1 22.3 %copy-start.1 = (f32[48,512]{1,0:T(8,128)S(1)}, f32[48,512]{1,0:T(8,128)}, u32[]{:S(2)}) copy-start(f32[48,512]{1,0:T(8,128)} %param.5) | copy-start | bytes 294916
  28.6 23.1 %copy-start.2 = (s32[48]{0:T(128)S(1)}, s32[48]{0:T(128)}, u32[]{:S(2)}) copy-start(s32[48]{0:T(128)} %param.6) | copy-start | bytes 580
Sparse Core Ops, SparseCore 0:
  51.8 52.0 all-reduce.1
where the time goes:
time: 167 us; the launch traced here: 166 us
  blocking collectives  85 us (51%)
  waiting for transfers between devices  48.8 us (29%)
  between operations  14.1 us (8%)
  other arithmetic  9.08 us (5%)
  local copies, waits for them, and re-layouts  7.22 us (4%)
  matrix products  2.06 us (1%)
    psum x1, waiting for transfers between devices, on_device(): summed = lax.psum(partial_value, 'row')  48.8 us
    psum x1, blocking collectives, on_device(): total = lax.psum(jnp.sum(emitted, axis=1), ('row', 'col'))  39.3 us
    all_gather x1, blocking collectives, on_device(): next_alpha = lax.all_gather(scaled, 'col', axis=1, tiled=True)  13.3 us
    pmax x1, blocking collectives, on_device(): row_peak = lax.pmax(local_peak, 'col')  12.1 us
    all_gather x1, blocking collectives, on_device(): lax.all_gather(dst_emb, 'row', axis=1, tiled=True)  11.9 us
    psum x1, blocking collectives, on_device(): row_total = lax.psum(local_total * jnp.exp(local_peak - row_peak), 'col')  8.37 us
    gather x1, local copies, waits for them, and re-layouts, on_device(): emit_rows = jnp.take(emission, tokens, axis=0).astype(jnp.float32)  3.35 us
  transfers between devices with their start and end apart: 1, of which 1 were waited for; matrix products, arithmetic and copies ran while one was open for 2% of the time, Pallas kernels for 0%

commit v1 on v0

--- a/solution.py
+++ b/solution.py
@@ -80,7 +80,7 @@
     partial_value = lax.fori_loop(
         0, local_groups // per_block, multiply, jnp.zeros((seq_count, tile_cols), jnp.float32)
     )
-    summed = lax.psum(partial_value, "row")
+    summed = jnp.sum(lax.all_gather(partial_value, "row"), axis=0)
     own_sums = lax.dynamic_slice_in_dim(summed, row_index * group_cols, group_cols, 1)
     emit_rows = jnp.take(emission, tokens, axis=0).astype(jnp.float32)
     emitted = own_sums * emit_rows

time: 167 us -> 139 us (0.83)
  waiting for transfers between devices: 48.8 us -> 21.1 us
    psum x1 -> x0, waiting for transfers between devices: 48.8 us -> none  [on_device(): summed = lax.psum(partial_value, 'row')]
    all_gather x0 -> x1, waiting for transfers between devices: none -> 21.1 us  [on_device(): summed = jnp.sum(lax.all_gather(partial_value, 'row'), axis=0)]
where the time goes in v1:
time: 139 us
  blocking collectives  85 us (61%)
  waiting for transfers between devices  21.1 us (15%)
  between operations  14.1 us (10%)
  other arithmetic  9.13 us (7%)
  local copies, waits for them, and re-layouts  7.3 us (5%)
  matrix products  2.06 us (1%)
    psum x1, blocking collectives, on_device(): total = lax.psum(jnp.sum(emitted, axis=1), ('row', 'col'))  39.3 us
    all_gather x1, waiting for transfers between devices, on_device(): summed = jnp.sum(lax.all_gather(partial_value, 'row'), axis=0)  21.1 us
    all_gather x1, blocking collectives, on_device(): next_alpha = lax.all_gather(scaled, 'col', axis=1, tiled=True)  13.3 us
    pmax x1, blocking collectives, on_device(): row_peak = lax.pmax(local_peak, 'col')  12.1 us
    all_gather x1, blocking collectives, on_device(): lax.all_gather(dst_emb, 'row', axis=1, tiled=True)  11.9 us
    psum x1, blocking collectives, on_device(): row_total = lax.psum(local_total * jnp.exp(local_peak - row_peak), 'col')  8.37 us
    gather x1, local copies, waits for them, and re-layouts, on_device(): emit_rows = jnp.take(emission, tokens, axis=0).astype(jnp.float32)  3.35 us
    reduce_sum x1, other arithmetic, absorb_block(): block_total = jnp.sum(shifted, axis=2)  2.81 us
  transfers between devices with their start and end apart: 1, of which 1 were waited for; matrix products, arithmetic and copies ran while one was open for 2% of the time, Pallas kernels for 0%

profile of v1, /device:TPU:0, one launch (start us, length us, event | category | flops | bytes accessed | tf_op | source)
XLA Modules:
  0.0 138.8 jit_solution(12344336109398088085)
XLA Ops:
  7.2 0.0 copy-start
  7.2 0.0 all-gather.2.cloned.1.call-start
  7.2 11.9 %all_gather.12 = bf16[256,1024]{1,0:T(8,128)(2,1)S(1)} all-gather(bf16[256,128]{1,0:T(8,128)(2,1)} %param.8), channel_id=1, replica_groups=mesh['row'=8,'col'=4] {'row'}, dimensions={1}, use_global_device_ids=true | all-gather | bytes 589824 | tf_op jit(solution)/shard_map/all_gather | solution.py:52
  19.1 0.0 copy-done
  19.1 0.4 fusion.11
  19.5 1.8 %copy.19 = f32[64,8,8,128]{3,2,1,0:T(8,128)} copy(f32[64,8,8,128]{3,1,2,0:T(8,128)S(1)} %bitcast.22) | data formatting | bytes 4194304
  21.4 2.2 %reduce_max.19 = f32[512,8]{1,0:T(8,128)S(1)} reduce(f32[512,8,128]{2,1,0:T(8,128)} %bitcast.23, f32[]{:T(128)} %constant.29.clone.1), dimensions={2}, to_apply=%region_0.1 | reduce | flops 520192 | bytes 2113540 | tf_op jit(solution)/shard_map/while/body/eval_jaxpr/reduce_max | solution.py:20
  23.6 2.8 %exponential_reduce_fusion = f32[512,8]{1,0:T(8,128)S(1)} fusion(f32[512,8,128]{2,1,0:T(8,128)} %bitcast.24, f32[512,8]{1,0:T(8,128)S(1)} %reduce_max.19), kind=kLoop, calls=%fused_computation.4 | loop fusion | flops 1044480 | bytes 2129920 | tf_op jit(solution)/shard_map/while/body/eval_jaxpr/reduce_sum | solution.py:22
  26.4 0.1 copy.15
  26.5 0.6 sub.38
  27.1 0.0 copy-start.1
  27.1 1.5 %fusion.9 = (f32[512]{0:T(512)S(1)}, bf16[64,8,8,128]{3,2,1,0:T(8,128)(2,1)}) fusion(f32[512,1024]{1,0:T(8,128)S(1)} %fusion.11, f32[64,8,8,128]{3,2,1,0:T(8,128)S(1)} %bitcast.25), kind=kLoop, calls=%fused_computation.23 | loop fusion | flops 1572352 | bytes 5244928 | tf_op jit(solution)/shard_map/reduce_max | solution.py:57
  28.6 0.0 copy-start.2
  28.6 12.1 %pmax.7 = f32[512]{0:T(512)S(1)} all-reduce(f32[512]{0:T(512)S(1)} %get-tuple-element.29), channel_id=1, replica_groups=mesh['row'=8,'col'=4] {'col'}, use_global_device_ids=true, to_apply=%region_2.3 | all-reduce | flops 512 | bytes 4096 | tf_op jit(solution)/shard_map/pmax | solution.py:59
  40.7 0.2 multiply_reduce_fusion
  41.0 8.4 %psum.14 = f32[512]{0:T(512)S(1)} all-reduce(f32[512]{0:T(512)S(1)} %exponential_multiply_fusion), channel_id=1, replica_groups=mesh['row'=8,'col'=4] {'col'}, use_global_device_ids=true, to_apply=%region_5.0 | all-reduce | flops 512 | bytes 4096 | tf_op jit(solution)/shard_map/psum | solution.py:60
  49.4 0.0 copy-done.1
  49.4 1.6 %convolution_bitcast_fusion = f32[48,8,128]{2,0,1:T(8,128)S(1)} fusion(bf16[64,8,8,128]{3,2,1,0:T(8,128)(2,1)} %get-tuple-element.30, f32[48,512]{1,0:T(8,128)S(1)} %copy-done.1, f32[8,512]{1,0:T(8,128)S(1)} %divide_bitcast_fusion), kind=kOutput, calls=%fused_computation.5 | convolution fusion | flops 50724864 | bytes 1359872 | tf_op jit(solution)/shard_map/while/body/eval_jaxpr/gbi,igk->bgk/dot_general | solution.py:72
  51.0 0.1 copy.17
  51.1 0.7 all_gather.13
  51.8 0.0 all-gather.2.cloned.1.call-update
  51.8 0.0 copy-done.2
  51.8 3.3 %gather_fusion = bf16[48,128]{1,0:T(8,128)(2,1)S(1)} fusion(bf16[16640,128]{1,0:T(8,128)(2,1)} %param.9, s32[1024]{0:T(1024)S(1)} %pad_clamp_fusion), kind=kCustom, calls=%fused_computation | custom fusion | bytes 24768 | tf_op jit(solution)/shard_map/jit(_take)/gather | solution.py:85
  55.2 21.1 %all-gather.2.cloned.1.call-done = f32[8,48,1024]{2,1,0:T(8,128)} async-done(((f32[1,48,1024]{2,1,0:T(8,128)}), f32[8,48,1024]{2,1,0:T(8,128)}) %all-gather.2.cloned.1.call-update) | async-done | bytes 1572880 | tf_op jit(solution)/shard_map/all_gather | solution.py:83
  76.3 1.5 %reduce_sum.39 = f32[48,1024]{1,0:T(8,128)S(1)} reduce(f32[8,48,1024]{2,1,0:T(8,128)} %all-gather.2.cloned.1.call-done, f32[]{:T(128)} %constant.35.clone.1), dimensions={0}, to_apply=%region_6.0 | reduce | flops 344064 | bytes 1769476 | tf_op jit(solution)/shard_map/reduce_sum | solution.py:83
  77.9 0.2 fusion.8
  78.0 39.3 %psum.15 = f32[48]{0:T(128)S(1)} all-reduce(f32[48]{0:T(128)S(1)} %fusion.8), channel_id=1, replica_groups=mesh['row'=8,'col'=4] {'row','col'}, use_global_device_ids=true, to_apply=%region_8.0 | all-reduce | flops 48 | bytes 384 | tf_op jit(solution)/shard_map/psum | solution.py:88
  117.4 0.5 fusion.10
  117.9 0.1 fusion.7
  118.0 13.3 %all_gather.15 = f32[48,512]{1,0:T(8,128)S(1)} all-gather(f32[48,128]{1,0:T(8,128)S(1)} %fusion.7), channel_id=1, replica_groups=mesh['row'=8,'col'=4] {'col'}, dimensions={1}, use_global_device_ids=true | all-gather | bytes 122880 | tf_op jit(solution)/shard_map/all_gather | solution.py:90
  131.3 0.6 copy.29
  (5 shorter events, 0.0 us)
Async XLA Ops:
  7.2 11.9 %copy-start = (bf16[512,256]{1,0:T(8,128)(2,1)S(1)}, bf16[512,256]{1,0:T(8,128)(2,1)}, u32[]{:S(2)}) copy-start(bf16[512,256]{1,0:T(8,128)(2,1)} %param.7) | copy-start | bytes 786436
  7.2 69.2 %all-gather.2.cloned.1.call-start = ((), (), s32[]{:S(2)}) async-start(), calls=%async_computation | async-start | bytes 1769472 | tf_op jit(solution)/shard_map/all_gather | solution.py:83
  27.1 22.3 %copy-start.1 = (f32[48,512]{1,0:T(8,128)S(1)}, f32[48,512]{1,0:T(8,128)}, u32[]{:S(2)}) copy-start(f32[48,512]{1,0:T(8,128)} %param.5) | copy-start | bytes 294916
  28.6 23.2 %copy-start.2 = (s32[48]{0:T(128)S(1)}, s32[48]{0:T(128)}, u32[]{:S(2)}) copy-start(s32[48]{0:T(128)} %param.6) | copy-start | bytes 580
Sparse Core Ops, SparseCore 0:
  51.9 24.3 all-gather.1
